TPU v7x, 32 devices: a whole 2x2x4 slice. The times are simulated.
32 devices in a mesh: dist: 4 (over y, x), rows: 8 (over z, core).
Axes of the slice: x: 2, y: 2, z: 4, core: 2. Of those that a mesh axis runs over, the one named last changes fastest.
Arguments:
- volume: bfloat16 [128, 128, 2048], P('rows', None, 'dist'), may hold values from -6 to 6
- kernels: bfloat16 [128, 2, 128, 128], P('rows'), may hold values from -0.09375 to 0.09375
- targets: int32 [128, 2], P('rows'), may hold values from 0 to 7, all different within a row; in each aligned block of 16 rows (0 to 15, 16 to 31, ...) at most 8 rows name the same one
- contrast: bfloat16 [4, 8, 128, 2048], P('dist', 'rows'), may hold values from -6 to 6
- fresnel_numbers: float32 [4], P('dist'), may hold values from 0.4 to 1.6
Outputs:
- gradient: bfloat16 [128, 128, 2048], P('rows', None, 'dist')
Inputs may be any that keep to these rules, and one draw needn't show every extreme that they name: `targets`: each row names 2 different detector blocks; among the rows of one index of rows no detector block is named more than 8 times, and some block is named exactly 8 times.
All inputs are finite; a program needn't handle non-finite values.
Results may differ from a plain program's by a relative error of at most 0.0063.
Values may be sent and summed in bfloat16 or wider, within the bound.
No kernel may reach another device: no remote copies, remote signals or barrier semaphores. Data moves between devices by JAX's collectives and lax.ppermute only.
A program may use at most 128 MiB of HBM per device.

v0:
```python
import math
import jax
import jax.numpy as jnp
from jax import lax
from jax.sharding import PartitionSpec as P


def spectral_table(width):
    half = width // 2
    index_rows = lax.broadcasted_iota(jnp.int32, (width, half), 0)
    index_cols = lax.broadcasted_iota(jnp.int32, (width, half), 1) + 1
    turns = (index_rows * index_cols % width).astype(jnp.float32) * (2.0 * math.pi / width)
    return jnp.concatenate([jnp.cos(turns), jnp.sin(turns)], axis=1)


def spectral_weight(width, number):
    half = width // 2
    freq = (lax.iota(jnp.int32, half) + 1).astype(jnp.float32)
    factor = jnp.sin(jnp.pi * number * freq * freq / width)
    scaled = factor * jnp.where(freq < half, 2.0, 1.0) / width
    return jnp.concatenate([scaled, scaled])


def shards(volume, kernels, targets, contrast, fresnel_numbers):
    owners = lax.axis_size("rows")
    vblocks, blk, quarter = volume.shape
    top = kernels.shape[1]
    items = vblocks * top
    width = contrast.shape[-1]
    contrib = jnp.einsum("btij,bjw->btiw", kernels, volume, preferred_element_type=jnp.float32)
    contrib = contrib.astype(jnp.bfloat16).reshape(items, blk * quarter)
    flat = targets.reshape(items)
    capacity = max(2, 2 * items // owners)
    later = lax.broadcasted_iota(jnp.int32, (items, items), 0)
    before = lax.broadcasted_iota(jnp.int32, (items, items), 1)
    same = (flat[:, None] == flat[None, :]) & (before < later)
    rank = jnp.sum(same.astype(jnp.int32), axis=1)
    slot = flat * capacity + rank
    place = (
        slot[None, :] == lax.broadcasted_iota(jnp.int32, (owners * capacity, items), 0)
    ).astype(jnp.bfloat16)
    outgoing = jnp.dot(place, contrib, preferred_element_type=jnp.float32).astype(jnp.bfloat16)
    outgoing = outgoing.reshape(owners, capacity, blk, quarter)
    arrived = lax.all_to_all(outgoing, "rows", split_axis=0, concat_axis=0, tiled=True)
    per_owner = jnp.sum(arrived.astype(jnp.float32), axis=1).astype(jnp.bfloat16)
    projection = jnp.sum(per_owner.astype(jnp.float32), axis=0)
    table = spectral_table(width)
    weight = spectral_weight(width, fresnel_numbers[0])
    spectrum = jnp.dot(
        lax.all_gather(projection, "dist", axis=1, tiled=True),
        table,
        precision=lax.Precision.HIGHEST,
        preferred_element_type=jnp.float32,
    )

    def synthesize(coeffs):
        return lax.dot_general(
            coeffs * weight,
            table,
            (((1,), (1,)), ((), ())),
            precision=lax.Precision.HIGHEST,
            preferred_element_type=jnp.float32,
        )

    residual = -2.0 * synthesize(spectrum) - contrast[0, 0].astype(jnp.float32)
    analysed = jnp.dot(
        residual, table, precision=lax.Precision.HIGHEST, preferred_element_type=jnp.float32
    )
    term = -2.0 * synthesize(analysed)
    summed = lax.psum(term, "dist")
    own_cols = lax.dynamic_slice_in_dim(summed, lax.axis_index("dist") * quarter, quarter, 1)
    image_gradient = own_cols.astype(jnp.bfloat16)
    piece = lax.all_gather(image_gradient[None], "rows", axis=0, tiled=True)
    count = piece.shape[0]
    pick = (flat[:, None] == lax.broadcasted_iota(jnp.int32, (items, count), 1)).astype(
        jnp.bfloat16
    )
    gathered = jnp.dot(
        pick, piece.reshape(count, blk * quarter), preferred_element_type=jnp.float32
    )
    chosen = gathered.astype(jnp.bfloat16).reshape(vblocks, top, blk, quarter)
    grad = jnp.einsum("btij,btiw->bjw", kernels, chosen, preferred_element_type=jnp.float32)
    return grad.astype(jnp.bfloat16)


def solution(mesh):
    in_specs = (
        P("rows", None, "dist"),
        P("rows", None, None, None),
        P("rows", None),
        P("dist", "rows", None, None),
        P("dist"),
    )
    out_specs = P("rows", None, "dist")
    return jax.shard_map(shards, mesh=mesh, in_specs=in_specs, out_specs=out_specs, check_vma=False)
```

profile of v0, /device:TPU:0, one launch (start us, length us, event | category | flops | bytes accessed | tf_op | source)
XLA Modules:
  0.0 398.6 jit_solution(16857438083517022711)
XLA Ops:
  6.5 0.0 copy-start
  6.5 0.0 all-gather.4.cloned.1.call-start
  6.5 0.9 copy.12
  7.4 0.1 eq.33
  7.5 0.2 convert_reduce_fusion.1
  7.7 0.4 copy-done
  8.1 2.5 convolution_convert_fusion.2
  10.6 2.4 copy.18
  13.0 2.3 convolution_convert_fusion
  15.3 190.8 %all_to_all.5 = bf16[8,8,128,512]{3,1,2,0:T(8,128)(2,1)} all-to-all(bf16[8,8,128,512]{3,1,2,0:T(8,128)(2,1)S(1)} %bitcast.32), channel_id=1, replica_groups=mesh['dist'=4,'rows'=8] {'rows'}, dimensions={0} | all-to-all | bytes 16777216 | tf_op jit(solution)/shard_map/all_to_all | solution.py:44
  206.1 9.2 %reduce_sum.31 = bf16[8,128,512]{2,1,0:T(8,128)(2,1)S(1)} reduce(bf16[8,8,128,512]{3,1,2,0:T(8,128)(2,1)} %all_to_all.5, bf16[]{:T(256)} %constant.18.clone.1), dimensions={1}, to_apply=%region_1.0 | reduce | flops 3670016 | bytes 9437186 | tf_op jit(solution)/shard_map/reduce_sum | solution.py:45
  215.3 0.8 convert_reduce_fusion
  216.2 0.0 all-gather.4.cloned.1.call-update
  216.2 0.6 all-gather.6.cloned.1.call-start
  217.5 0.1 fusion.25
  217.5 34.4 %fusion.11 = (f32[2048,1024]{1,0:T(8,128)}, f32[2048,1024]{1,0:T(8,128)}) fusion(s32[1024]{0:T(1024)S(1)} %iota_add_fusion), kind=kLoop, calls=%fused_computation.18 | loop fusion | flops 29360128 | bytes 16781312 | tf_op jit(solution)/shard_map/cos | solution.py:13
  251.9 0.0 all-gather.4.cloned.1.call-done
  251.9 0.0 copy-start.2
  251.9 0.0 copy-start.4
  252.0 15.1 %fusion.12 = f32[128,2048]{1,0:T(8,128)S(1)} fusion(f32[128,2048]{1,0:T(8,128)} %all-gather.4.cloned.1.call-done, f32[2048,1024]{1,0:T(8,128)} %get-tuple-element.6, f32[2048,1024]{1,0:T(8,128)} %get-tuple-element.5, f32[2048]{0:T(1024)S(1)} %pad_maximum_fusion.15), kind=kOutput, calls=%fused_computation.20 | convolution fusion | flops 6446907392 | bytes 18882560 | tf_op jit(solution)/shard_map/dot_general | solution.py:49
  267.1 0.0 copy-done.2
  267.1 0.0 copy-done.4
  267.1 19.9 %fusion.16 = f32[128,2048]{1,0:T(8,128)S(1)} fusion(f32[128,2048]{1,0:T(8,128)S(1)} %fusion.12, f32[2048,1024]{1,0:T(8,128)} %get-tuple-element.6, f32[2048,1024]{1,0:T(8,128)S(1)} %copy-done.2, bf16[1,1,128,2048]{3,2,1,0:T(8,128)(2,1)S(1)} %copy-done.4), kind=kOutput, calls=%fused_computation.24 | convolution fusion | flops 6447431680 | bytes 19398656 | tf_op jit(solution)/shard_map/dot_general | solution.py:57
  287.0 11.0 %fusion.14 = f32[128,2048]{1,0:T(8,128)S(1)} fusion(f32[128,2048]{1,0:T(8,128)S(1)} %fusion.16, f32[2048,1024]{1,0:T(8,128)} %get-tuple-element.6, f32[2048,1024]{1,0:T(8,128)S(1)} %copy-done.2, f32[2048]{0:T(1024)S(1)} %pad_maximum_fusion.15), kind=kOutput, calls=%fused_computation.22 | convolution fusion | flops 6446907392 | bytes 18882560 | tf_op jit(solution)/shard_map/dot_general | solution.py:66
  297.9 19.9 %fusion.15 = f32[128,2048]{1,0:T(8,128)S(1)} fusion(f32[128,2048]{1,0:T(8,128)S(1)} %fusion.14, f32[2048,1024]{1,0:T(8,128)} %get-tuple-element.6, f32[2048,1024]{1,0:T(8,128)S(1)} %copy-done.2), kind=kOutput, calls=%fused_computation.23 | convolution fusion | flops 6446907392 | bytes 18874368 | tf_op jit(solution)/shard_map/dot_general | solution.py:57
  317.8 41.1 %all-reduce.1 = bf16[128,2048]{1,0:T(8,128)(2,1)S(1)} all-reduce(f32[128,2048]{1,0:T(8,128)S(1)} %fusion.15), channel_id=1, replica_groups=mesh['dist'=4,'rows'=8] {'dist'}, use_global_device_ids=true, to_apply=%region_3.4 | all-reduce | flops 262144 | bytes 1572864 | tf_op jit(solution)/shard_map/psum | solution.py:70
  358.9 0.0 copy-start.3
  358.9 0.7 dynamic-slice_convert_fusion
  359.6 0.0 all-gather.6.cloned.1.call-update
  359.6 20.7 %all-gather.6.cloned.1.call-done = bf16[1024,512]{1,0:T(8,128)(2,1)} async-done(((bf16[128,512]{1,0:T(8,128)(2,1)}), bf16[1024,512]{1,0:T(8,128)(2,1)}) %all-gather.6.cloned.1.call-update) | async-done | bytes 1048592 | tf_op jit(solution)/shard_map/all_gather | solution.py:73
  380.3 1.7 reshape.30
  382.0 1.3 convolution_convert_fusion.1
  383.3 0.0 copy-start.1
  383.3 1.5 copy.19
  384.9 0.0 copy-done.3
  384.9 2.8 fusion.18
  387.6 3.9 copy.14
  391.5 0.0 copy-done.1
  (3 shorter events, 0.0 us)
Async XLA Ops:
  6.5 1.6 copy-start
  6.5 245.4 %all-gather.4.cloned.1.call-start = ((), (), s32[]{:S(2)}) async-start(), calls=%async_computation.1 | async-start | bytes 1310720 | tf_op jit(solution)/shard_map/all_gather | solution.py:50
  216.2 164.1 %all-gather.6.cloned.1.call-start = ((), (), s32[]{:S(2)}) async-start(), calls=%async_computation.2 | async-start | bytes 1179648 | tf_op jit(solution)/shard_map/all_gather | solution.py:73
  251.9 15.1 %copy-start.2 = (f32[2048,1024]{1,0:T(8,128)S(1)}, f32[2048,1024]{1,0:T(8,128)}, u32[]{:S(2)}) copy-start(f32[2048,1024]{1,0:T(8,128)} %get-tuple-element.5) | copy-start | bytes 25165828
  251.9 15.1 %copy-start.4 = (bf16[1,1,128,2048]{3,2,1,0:T(8,128)(2,1)S(1)}, bf16[1,1,128,2048]{3,2,1,0:T(8,128)(2,1)}, u32[]{:S(2)}) copy-start(bf16[1,1,128,2048]{3,2,1,0:T(8,128)(2,1)} %param.8) | copy-start | bytes 1572868
  358.9 25.9 %copy-start.3 = (bf16[16,2,128,128]{3,2,1,0:T(8,128)(2,1)S(1)}, bf16[16,2,128,128]{3,2,1,0:T(8,128)(2,1)}, u32[]{:S(2)}) copy-start(bf16[16,2,128,128]{3,2,1,0:T(8,128)(2,1)} %param.6) | copy-start | bytes 3145732
  383.3 8.2 %copy-start.1 = (bf16[16,128,512]{2,1,0:T(8,128)(2,1)S(1)}, bf16[16,128,512]{2,1,0:T(8,128)(2,1)}, u32[]{:S(2)}) copy-start(bf16[16,128,512]{2,1,0:T(8,128)(2,1)} %param.5) | copy-start | bytes 6291460
Sparse Core Ops, SparseCore 0:
  216.3 25.1 all-gather.3
  359.7 20.5 all-gather.5
where the time goes:
time: 404 us; the launch traced here: 399 us
  blocking collectives  232 us (57%)
  matrix products  74.6 us (18%)
  other arithmetic  44.7 us (11%)
  waiting for transfers between devices  20.7 us (5%)
  between operations  14.5 us (4%)
  local copies, waits for them, and re-layouts  11.7 us (3%)
    all_to_all x1, blocking collectives, shards(): lax.all_to_all(outgoing, 'rows', split_axis=0, concat_axis=0, tiled=True)  191 us
    psum x1, blocking collectives, shards(): summed = lax.psum(term, 'dist')  41.1 us
    dot_general x2, matrix products, synthesize(): lax.dot_general(coeffs * weight, table, (((1,), (1,)), ((), ())), precisi...  39.7 us
    cos x1, other arithmetic, spectral_table(): return jnp.concatenate([jnp.cos(turns), jnp.sin(turns)], axis=1)  34.4 us
    all_gather x1, waiting for transfers between devices, shards(): piece = lax.all_gather(image_gradient[None], 'rows', axis=0, tiled=True)  20.7 us
    dot_general x1, matrix products, shards(): jnp.dot(lax.all_gather(projection, 'dist', axis=1, tiled=True), table, pr...  15.1 us
    dot_general x1, matrix products, shards(): jnp.dot(residual, table, precision=lax.Precision.HIGHEST, preferred_eleme...  11 us
    reduce_sum x1, other arithmetic, shards(): jnp.sum(arrived.astype(jnp.float32), axis=1).astype(jnp.bfloat16)  9.19 us
  transfers between devices with their start and end apart: 2, of which 1 were waited for; matrix products, arithmetic and copies ran while one was open for 9% of the time, Pallas kernels for 0%

commit v1 on v0

--- a/solution.py
+++ b/solution.py
@@ -70,7 +70,26 @@
     summed = lax.psum(term, "dist")
     own_cols = lax.dynamic_slice_in_dim(summed, lax.axis_index("dist") * quarter, quarter, 1)
     image_gradient = own_cols.astype(jnp.bfloat16)
-    piece = lax.all_gather(image_gradient[None], "rows", axis=0, tiled=True)
+    ways, here, step = (
+        lax.axis_size("rows"),
+        lax.axis_index("rows"),
+        image_gradient[None].shape[0],
+    )
+    lengths = [n * ways if d == 0 else n for d, n in enumerate(image_gradient[None].shape)]
+    piece = lax.dynamic_update_slice_in_dim(
+        jnp.zeros(lengths, image_gradient[None].dtype), image_gradient[None], here * step, axis=0
+    )
+    going_up = going_down = image_gradient[None]
+    for far in range(1, ways // 2 + 1):
+        going_up = lax.ppermute(going_up, "rows", [(d, (d + 1) % ways) for d in range(ways)])
+        piece = lax.dynamic_update_slice_in_dim(piece, going_up, (here - far) % ways * step, axis=0)
+        if 2 * far < ways:
+            going_down = lax.ppermute(
+                going_down, "rows", [(d, (d - 1) % ways) for d in range(ways)]
+            )
+            piece = lax.dynamic_update_slice_in_dim(
+                piece, going_down, (here + far) % ways * step, axis=0
+            )
     count = piece.shape[0]
     pick = (flat[:, None] == lax.broadcasted_iota(jnp.int32, (items, count), 1)).astype(
         jnp.bfloat16

time: 404 us -> 408 us (level)
  starting transfers between devices: 0.63 us -> 11 us
  waiting for transfers between devices: 20.7 us -> 15.4 us
    all_gather x1 -> x0, waiting for transfers between devices: 20.7 us -> none  [shards(): piece = lax.all_gather(image_gradient[None], 'rows', axis=0, tiled=True)]
    ppermute x0 -> x7, waiting for transfers between devices: none -> 15.4 us  [the longest x4 15.4 us: shards(): lax.ppermute(going_up, 'rows', [(d, (d + 1) % ways) for d in range(ways)])]
    ppermute x0 -> x7, starting transfers between devices: none -> 11 us  [the longest x3 10.6 us: shards(): lax.ppermute(going_down, 'rows', [(d, (d - 1) % ways) for d in range(ways)])]
  transfers between devices with their start and end apart: 2 -> 8, of which waited for: 1 -> 4; matrix products, arithmetic and copies ran while one was open for 9% -> 9% of each run, Pallas kernels for 0% -> 0%
where the time goes in v1:
time: 408 us; the launch traced here: 403 us
  blocking collectives  232 us (57%)
  matrix products  74.7 us (18%)
  other arithmetic  44.8 us (11%)
  waiting for transfers between devices  15.4 us (4%)
  between operations  14.8 us (4%)
  starting transfers between devices  11 us (3%)
  local copies, waits for them, and re-layouts  10.1 us (2%)
    all_to_all x1, blocking collectives, shards(): lax.all_to_all(outgoing, 'rows', split_axis=0, concat_axis=0, tiled=True)  191 us
    psum x1, blocking collectives, shards(): summed = lax.psum(term, 'dist')  40.8 us
    dot_general x2, matrix products, synthesize(): lax.dot_general(coeffs * weight, table, (((1,), (1,)), ((), ())), precisi...  39.8 us
    cos x1, other arithmetic, spectral_table(): return jnp.concatenate([jnp.cos(turns), jnp.sin(turns)], axis=1)  34.6 us
    ppermute x4, waiting for transfers between devices, shards(): lax.ppermute(going_up, 'rows', [(d, (d + 1) % ways) for d in range(ways)])  15.4 us
    dot_general x1, matrix products, shards(): jnp.dot(lax.all_gather(projection, 'dist', axis=1, tiled=True), table, pr...  15.1 us
    dot_general x1, matrix products, shards(): jnp.dot(residual, table, precision=lax.Precision.HIGHEST, preferred_eleme...  11 us
    ppermute x3, starting transfers between devices, shards(): lax.ppermute(going_down, 'rows', [(d, (d - 1) % ways) for d in range(ways)])  10.6 us
  transfers between devices with their start and end apart: 8, of which 4 were waited for; matrix products, arithmetic and copies ran while one was open for 9% of the time, Pallas kernels for 0%

profile of v1, /device:TPU:0, one launch (start us, length us, event | category | flops | bytes accessed | tf_op | source)
XLA Modules:
  0.0 402.6 jit_solution(13090835304808231746)
XLA Ops:
  6.5 0.0 copy-start
  6.5 0.0 all-gather.2.cloned.1.call-start
  6.5 0.9 copy.12
  7.4 0.1 eq.41
  7.5 0.2 convert_reduce_fusion.1
  7.7 0.4 copy-done
  8.1 2.5 convolution_convert_fusion.2
  10.6 2.4 copy.18
  13.0 2.3 convolution_convert_fusion
  15.3 191.0 %all_to_all.5 = bf16[8,8,128,512]{3,1,2,0:T(8,128)(2,1)} all-to-all(bf16[8,8,128,512]{3,1,2,0:T(8,128)(2,1)S(1)} %bitcast.37), channel_id=1, replica_groups=mesh['dist'=4,'rows'=8] {'rows'}, dimensions={0} | all-to-all | bytes 16777216 | tf_op jit(solution)/shard_map/all_to_all | solution.py:44
  206.3 9.2 %reduce_sum.31 = bf16[8,128,512]{2,1,0:T(8,128)(2,1)S(1)} reduce(bf16[8,8,128,512]{3,1,2,0:T(8,128)(2,1)} %all_to_all.5, bf16[]{:T(256)} %constant.78.clone.1), dimensions={1}, to_apply=%region_1.0 | reduce | flops 3670016 | bytes 9437186 | tf_op jit(solution)/shard_map/reduce_sum | solution.py:45
  215.5 0.8 convert_reduce_fusion
  216.4 0.0 all-gather.2.cloned.1.call-update
  217.0 0.1 fusion.26
  217.1 34.6 %fusion.11 = (f32[2048,1024]{1,0:T(8,128)}, f32[2048,1024]{1,0:T(8,128)}) fusion(s32[1024]{0:T(1024)S(1)} %iota_add_fusion), kind=kLoop, calls=%fused_computation.18 | loop fusion | flops 29360128 | bytes 16781312 | tf_op jit(solution)/shard_map/cos | solution.py:13
  251.7 0.0 all-gather.2.cloned.1.call-done
  251.7 0.0 copy-start.2
  251.7 0.0 copy-start.4
  251.7 15.1 %fusion.12 = f32[128,2048]{1,0:T(8,128)S(1)} fusion(f32[128,2048]{1,0:T(8,128)} %all-gather.2.cloned.1.call-done, f32[2048,1024]{1,0:T(8,128)} %get-tuple-element.8, f32[2048,1024]{1,0:T(8,128)} %get-tuple-element.7, f32[2048]{0:T(1024)S(1)} %pad_maximum_fusion.15), kind=kOutput, calls=%fused_computation.20 | convolution fusion | flops 6446907392 | bytes 18882560 | tf_op jit(solution)/shard_map/dot_general | solution.py:49
  266.8 0.0 copy-done.2
  266.9 0.0 copy-done.4
  266.9 19.9 %fusion.16 = f32[128,2048]{1,0:T(8,128)S(1)} fusion(f32[128,2048]{1,0:T(8,128)S(1)} %fusion.12, f32[2048,1024]{1,0:T(8,128)} %get-tuple-element.8, f32[2048,1024]{1,0:T(8,128)S(1)} %copy-done.2, bf16[1,1,128,2048]{3,2,1,0:T(8,128)(2,1)S(1)} %copy-done.4), kind=kOutput, calls=%fused_computation.24 | convolution fusion | flops 6447431680 | bytes 19398656 | tf_op jit(solution)/shard_map/dot_general | solution.py:57
  286.8 11.0 %fusion.14 = f32[128,2048]{1,0:T(8,128)S(1)} fusion(f32[128,2048]{1,0:T(8,128)S(1)} %fusion.16, f32[2048,1024]{1,0:T(8,128)} %get-tuple-element.8, f32[2048,1024]{1,0:T(8,128)S(1)} %copy-done.2, f32[2048]{0:T(1024)S(1)} %pad_maximum_fusion.15), kind=kOutput, calls=%fused_computation.22 | convolution fusion | flops 6446907392 | bytes 18882560 | tf_op jit(solution)/shard_map/dot_general | solution.py:66
  297.8 19.9 %fusion.15 = f32[128,2048]{1,0:T(8,128)S(1)} fusion(f32[128,2048]{1,0:T(8,128)S(1)} %fusion.14, f32[2048,1024]{1,0:T(8,128)} %get-tuple-element.8, f32[2048,1024]{1,0:T(8,128)S(1)} %copy-done.2), kind=kOutput, calls=%fused_computation.23 | convolution fusion | flops 6446907392 | bytes 18874368 | tf_op jit(solution)/shard_map/dot_general | solution.py:57
  317.7 40.8 %all-reduce.1 = bf16[128,2048]{1,0:T(8,128)(2,1)S(1)} all-reduce(f32[128,2048]{1,0:T(8,128)S(1)} %fusion.15), channel_id=1, replica_groups=mesh['dist'=4,'rows'=8] {'dist'}, use_global_device_ids=true, to_apply=%region_3.4 | all-reduce | flops 262144 | bytes 1572864 | tf_op jit(solution)/shard_map/psum | solution.py:70
  358.5 0.1 broadcast_in_dim.18
  358.6 0.1 collective-permute-start
  358.7 3.5 collective-permute-start.1
  362.2 3.9 collective-permute-done
  366.1 0.0 collective-permute-start.2
  366.1 0.0 collective-permute-done.1
  366.1 3.5 collective-permute-start.3
  369.7 2.8 collective-permute-done.2
  372.5 0.0 collective-permute-start.4
  372.5 0.0 collective-permute-done.3
  372.5 3.5 collective-permute-start.5
  376.0 0.0 copy-start.3
  376.1 2.6 collective-permute-done.4
  378.7 0.3 collective-permute-start.6
  379.0 0.0 collective-permute-done.5
  379.0 6.1 %collective-permute-done.6 = bf16[1,128,512]{2,1,0:T(8,128)(2,1)S(1)} collective-permute-done((bf16[1,128,512]{2,1,0:T(8,128)(2,1)S(1)}, bf16[1,128,512]{2,1,0:T(8,128)(2,1)S(1)}, u32[]{:S(2)}, u32[]{:S(2)}) %collective-permute-start.6) | collective-permute-done | bytes 131104 | tf_op jit(solution)/shard_map/ppermute | solution.py:84
  385.1 0.6 copy.19
  385.7 1.3 convolution_convert_fusion.1
  387.0 0.0 copy-start.1
  387.0 1.5 copy.20
  388.6 2.7 fusion.18
  391.3 3.9 copy.14
  395.2 0.0 copy-done.1
  (12 shorter events, 0.1 us)
Async XLA Ops:
  6.5 1.6 copy-start
  6.5 245.2 %all-gather.2.cloned.1.call-start = ((), (), s32[]{:S(2)}) async-start(), calls=%async_computation.1 | async-start | bytes 1310720 | tf_op jit(solution)/shard_map/all_gather | solution.py:50
  251.7 15.1 %copy-start.2 = (f32[2048,1024]{1,0:T(8,128)S(1)}, f32[2048,1024]{1,0:T(8,128)}, u32[]{:S(2)}) copy-start(f32[2048,1024]{1,0:T(8,128)} %get-tuple-element.7) | copy-start | bytes 25165828
  251.7 15.1 %copy-start.4 = (bf16[1,1,128,2048]{3,2,1,0:T(8,128)(2,1)S(1)}, bf16[1,1,128,2048]{3,2,1,0:T(8,128)(2,1)}, u32[]{:S(2)}) copy-start(bf16[1,1,128,2048]{3,2,1,0:T(8,128)(2,1)} %param.8) | copy-start | bytes 1572868
  358.6 7.5 %collective-permute-start = (bf16[1,128,512]{2,1,0:T(8,128)(2,1)S(1)}, bf16[1,128,512]{2,1,0:T(8,128)(2,1)S(1)}, u32[]{:S(2)}, u32[]{:S(2)}) collective-permute-start(bf16[1,128,512]{2,1,0:T(8,128)(2,1)S(1)} %get-tuple-element.6), channel_id=1, source_target_pairs={{0,1},{1,2},{2,3},{3,4},{4,5},{5,6},{6,7},{7,0},{8,9},{9,10},{10,1... | collective-permute-start | bytes 393224 | tf_op jit(solution)/shard_map/ppermute | solution.py:84
  358.7 7.5 %collective-permute-start.1 = (bf16[1,128,512]{2,1,0:T(8,128)(2,1)S(1)}, bf16[1,128,512]{2,1,0:T(8,128)(2,1)S(1)}, u32[]{:S(2)}, u32[]{:S(2)}) collective-permute-start(bf16[1,128,512]{2,1,0:T(8,128)(2,1)S(1)} %get-tuple-element.6), channel_id=1, source_target_pairs={{0,7},{1,0},{2,1},{3,2},{4,3},{5,4},{6,5},{7,6},{8,15},{9,8},{10,9... | collective-permute-start | bytes 393224 | tf_op jit(solution)/shard_map/ppermute | solution.py:87
  366.1 6.3 %collective-permute-start.2 = (bf16[1,128,512]{2,1,0:T(8,128)(2,1)S(1)}, bf16[1,128,512]{2,1,0:T(8,128)(2,1)S(1)}, u32[]{:S(2)}, u32[]{:S(2)}) collective-permute-start(bf16[1,128,512]{2,1,0:T(8,128)(2,1)S(1)} %collective-permute-done), channel_id=1, source_target_pairs={{0,1},{1,2},{2,3},{3,4},{4,5},{5,6},{6,7},{7,0},{8,9},{9,10},{10,1... | collective-permute-start | bytes 393224 | tf_op jit(solution)/shard_map/ppermute | solution.py:84
  366.1 6.3 %collective-permute-start.3 = (bf16[1,128,512]{2,1,0:T(8,128)(2,1)S(1)}, bf16[1,128,512]{2,1,0:T(8,128)(2,1)S(1)}, u32[]{:S(2)}, u32[]{:S(2)}) collective-permute-start(bf16[1,128,512]{2,1,0:T(8,128)(2,1)S(1)} %collective-permute-done.1), channel_id=1, source_target_pairs={{0,7},{1,0},{2,1},{3,2},{4,3},{5,4},{6,5},{7,6},{8,15},{9,8},{10,9... | collective-permute-start | bytes 393224 | tf_op jit(solution)/shard_map/ppermute | solution.py:87
  372.5 6.2 %collective-permute-start.4 = (bf16[1,128,512]{2,1,0:T(8,128)(2,1)S(1)}, bf16[1,128,512]{2,1,0:T(8,128)(2,1)S(1)}, u32[]{:S(2)}, u32[]{:S(2)}) collective-permute-start(bf16[1,128,512]{2,1,0:T(8,128)(2,1)S(1)} %collective-permute-done.2), channel_id=1, source_target_pairs={{0,1},{1,2},{2,3},{3,4},{4,5},{5,6},{6,7},{7,0},{8,9},{9,10},{10,1... | collective-permute-start | bytes 393224 | tf_op jit(solution)/shard_map/ppermute | solution.py:84
  372.5 6.5 %collective-permute-start.5 = (bf16[1,128,512]{2,1,0:T(8,128)(2,1)S(1)}, bf16[1,128,512]{2,1,0:T(8,128)(2,1)S(1)}, u32[]{:S(2)}, u32[]{:S(2)}) collective-permute-start(bf16[1,128,512]{2,1,0:T(8,128)(2,1)S(1)} %collective-permute-done.3), channel_id=1, source_target_pairs={{0,7},{1,0},{2,1},{3,2},{4,3},{5,4},{6,5},{7,6},{8,15},{9,8},{10,9... | collective-permute-start | bytes 393224 | tf_op jit(solution)/shard_map/ppermute | solution.py:87
  376.0 12.5 %copy-start.3 = (bf16[16,2,128,128]{3,2,1,0:T(8,128)(2,1)S(1)}, bf16[16,2,128,128]{3,2,1,0:T(8,128)(2,1)}, u32[]{:S(2)}) copy-start(bf16[16,2,128,128]{3,2,1,0:T(8,128)(2,1)} %param.6) | copy-start | bytes 3145732
  378.7 6.5 %collective-permute-start.6 = (bf16[1,128,512]{2,1,0:T(8,128)(2,1)S(1)}, bf16[1,128,512]{2,1,0:T(8,128)(2,1)S(1)}, u32[]{:S(2)}, u32[]{:S(2)}) collective-permute-start(bf16[1,128,512]{2,1,0:T(8,128)(2,1)S(1)} %collective-permute-done.4), channel_id=1, source_target_pairs={{0,1},{1,2},{2,3},{3,4},{4,5},{5,6},{6,7},{7,0},{8,9},{9,10},{10,1... | collective-permute-start | bytes 393224 | tf_op jit(solution)/shard_map/ppermute | solution.py:84
  387.0 8.2 %copy-start.1 = (bf16[16,128,512]{2,1,0:T(8,128)(2,1)S(1)}, bf16[16,128,512]{2,1,0:T(8,128)(2,1)}, u32[]{:S(2)}) copy-start(bf16[16,128,512]{2,1,0:T(8,128)(2,1)} %param.5) | copy-start | bytes 6291460
Sparse Core Ops, SparseCore 0:
  216.5 25.1 all-gather.1
